TPU v7x, 32 devices: a whole 2x2x4 slice. The times are simulated.
32 devices in a mesh: vp: 16 (over z, y, x), op: 2 (over core).
Axes of the slice: x: 2, y: 2, z: 4, core: 2. Of those that a mesh axis runs over, the one named last changes fastest.
Arguments:
- multipliers: bfloat16 [2048, 131072], P('op', 'vp'), may hold values from -6 to 6
- integrals: bfloat16 [131072, 1024], P('vp'), may hold values from -0.0234375 to 0.0234375
- amplitudes: bfloat16 [2048, 131072], P('op', 'vp'), may hold values from -0.09375 to 0.09375
- slab_multipliers: bfloat16 [1024, 2048], P('vp', 'op'), may hold values from -6 to 6
- slab_amplitudes: bfloat16 [1024, 2048], P('vp', 'op'), may hold values from -0.09375 to 0.09375
- residual_rest: bfloat16 [1024, 2048], P('vp', 'op'), may hold values from -6 to 6
- occupied_energy: bfloat16 [2048], P('op'), may hold values from -2.5 to -0.5
- virtual_energy: bfloat16 [1024], P('vp'), may hold values from 1 to 4
Outputs:
- updated_multipliers: bfloat16 [1024, 2048], P('vp', 'op')
- pair_density: bfloat16 [1024, 131072], P('op', 'vp')
All inputs are finite; a program needn't handle non-finite values.
Results may differ from a plain program's by a relative error of at most 0.004.
Values may be sent and summed in bfloat16 or wider, within the bound.
No kernel may reach another device: no remote copies, remote signals or barrier semaphores. Data moves between devices by JAX's collectives and lax.ppermute only.
A program may use at most 192 MiB of HBM per device.

v0:
```python
import jax
import jax.numpy as jnp
from jax import lax
from jax.sharding import PartitionSpec as P


def renew_slab(current, ladder, rest, virtual, occupied):
    divisor = virtual.astype(jnp.float32)[:, None] - occupied.astype(jnp.float32)[None, :]
    renewed = current.astype(jnp.float32) + (ladder + rest.astype(jnp.float32)) / divisor
    return renewed.astype(jnp.bfloat16)


def local(
    multipliers,
    integrals,
    amplitudes,
    slab_multipliers,
    slab_amplitudes,
    residual_rest,
    occupied_energy,
    virtual_energy,
):
    ladder = lax.psum_scatter(
        lax.dot_general(
            integrals, multipliers, (((0,), (1,)), ((), ())), preferred_element_type=jnp.float32
        ),
        "vp",
        scatter_dimension=0,
        tiled=True,
    )
    renewed = renew_slab(slab_multipliers, ladder, residual_rest, virtual_energy, occupied_energy)
    every_new, every_amp = (
        lax.all_gather(renewed, "vp", axis=0, tiled=True),
        lax.all_gather(slab_amplitudes, "vp", axis=0, tiled=True),
    )
    first = jnp.dot(every_new, amplitudes, preferred_element_type=jnp.float32)
    density = lax.psum_scatter(
        first + jnp.dot(every_amp, multipliers, preferred_element_type=jnp.float32),
        "op",
        scatter_dimension=0,
        tiled=True,
    )
    return (renewed, density.astype(jnp.bfloat16))


def solution(mesh):
    placed = (
        P("op", "vp"),
        P("vp", None),
        P("op", "vp"),
        P("vp", "op"),
        P("vp", "op"),
        P("vp", "op"),
        P("op"),
        P("vp"),
    )
    return jax.shard_map(
        local, mesh=mesh, in_specs=placed, out_specs=(P("vp", "op"), P("op", "vp")), check_vma=False
    )
```

profile of v0, /device:TPU:0, one launch (start us, length us, event | category | flops | bytes accessed | tf_op | source)
XLA Modules:
  0.0 348.0 jit_solution(1127960146421359603)
XLA Ops:
  7.2 0.0 copy-start.3
  7.2 0.0 copy-start.2
  7.2 0.0 copy-start
  7.2 0.0 copy-start.1
  7.2 0.0 reduce-scatter.3.cloned.1.call-start
  7.3 23.8 %fusion = f32[1024,1024]{1,0:T(8,128)} fusion(bf16[8192,1024]{1,0:T(8,128)(2,1)} %param.9, bf16[1024,8192]{1,0:T(8,128)(2,1)} %param.8), kind=kOutput, calls=%fused_computation.2 | convolution fusion | flops 17179869184 | bytes 37748736 | tf_op jit(solution)/shard_map/dot_general | solution.py:24
  31.1 0.0 reduce-scatter.3.cloned.1.call-update
  31.1 0.0 all-gather.3.cloned.1.call-start
  31.2 0.0 copy-done.3
  31.2 0.0 copy-done.2
  31.2 98.0 %reduce-scatter.3.cloned.1.call-done = f32[64,1024]{1,0:T(8,128)} async-done(((f32[1024,1024]{1,0:T(8,128)}), f32[64,1024]{1,0:T(8,128)}) %reduce-scatter.3.cloned.1.call-update) | async-done | bytes 262160 | tf_op jit(solution)/shard_map/reduce_scatter | solution.py:23
  129.2 0.0 copy-done
  129.2 0.0 copy-done.1
  129.2 1.7 add_convert_fusion
  131.0 0.0 all-gather.3.cloned.1.call-update
  131.0 0.0 all-gather.5.cloned.1.call-start
  131.0 0.7 all-gather.5.cloned.1.call-update
  131.7 0.2 reduce-scatter.5.cloned.1.call-start
  131.9 60.6 %all-gather.3.cloned.1.call-done = bf16[1024,1024]{1,0:T(8,128)(2,1)} async-done(((bf16[64,1024]{1,0:T(8,128)(2,1)}), bf16[1024,1024]{1,0:T(8,128)(2,1)}) %all-gather.3.cloned.1.call-update) | async-done | bytes 2097168 | tf_op jit(solution)/shard_map/all_gather | solution.py:33
  192.5 27.4 %fusion.1 = f32[1024,8192]{1,0:T(8,128)} fusion(bf16[1024,1024]{1,0:T(8,128)(2,1)} %all-gather.3.cloned.1.call-done, bf16[1024,8192]{1,0:T(8,128)(2,1)} %param.10), kind=kOutput, calls=%fused_computation.3 | convolution fusion | flops 17179869184 | bytes 52428800 | tf_op jit(solution)/shard_map/dot_general | solution.py:36
  219.9 34.6 %all-gather.5.cloned.1.call-done = bf16[1024,1024]{1,0:T(8,128)(2,1)} async-done(((bf16[64,1024]{1,0:T(8,128)(2,1)}), bf16[1024,1024]{1,0:T(8,128)(2,1)}) %all-gather.5.cloned.1.call-update) | async-done | bytes 2097168 | tf_op jit(solution)/shard_map/all_gather | solution.py:34
  254.5 36.6 %convolution_add_fusion = f32[1024,8192]{1,0:T(8,128)} fusion(f32[1024,8192]{1,0:T(8,128)} %fusion.1, bf16[1024,1024]{1,0:T(8,128)(2,1)} %all-gather.5.cloned.1.call-done, bf16[1024,8192]{1,0:T(8,128)(2,1)} %param.8), kind=kOutput, calls=%fused_computation | convolution fusion | flops 17188257792 | bytes 85983232 | tf_op jit(solution)/shard_map/dot_general | solution.py:38
  291.1 0.0 reduce-scatter.5.cloned.1.call-update
  291.1 41.4 %reduce-scatter.5.cloned.1.call-done = f32[512,8192]{1,0:T(8,128)} async-done(((f32[1024,8192]{1,0:T(8,128)}), f32[512,8192]{1,0:T(8,128)}) %reduce-scatter.5.cloned.1.call-update) | async-done | bytes 16777232 | tf_op jit(solution)/shard_map/reduce_scatter | solution.py:37
  332.5 8.9 %convert_element_type.23 = bf16[512,8192]{1,0:T(8,128)(2,1)} convert(f32[512,8192]{1,0:T(8,128)} %reduce-scatter.5.cloned.1.call-done) | non-fusion elementwise | flops 4194304 | bytes 25165824 | tf_op jit(solution)/shard_map/convert_element_type | solution.py:43
  (2 shorter events, 0.0 us)
Async XLA Ops:
  7.2 24.0 %copy-start.3 = (bf16[64]{0:T(256)(128)(2,1)S(1)}, bf16[64]{0:T(256)(128)(2,1)}, u32[]{:S(2)}) copy-start(bf16[64]{0:T(256)(128)(2,1)} %param.15) | copy-start | bytes 388
  7.2 24.0 %copy-start.2 = (bf16[1024]{0:T(1024)(128)(2,1)S(1)}, bf16[1024]{0:T(1024)(128)(2,1)}, u32[]{:S(2)}) copy-start(bf16[1024]{0:T(1024)(128)(2,1)} %param.14) | copy-start | bytes 6148
  7.2 122.0 %copy-start = (bf16[64,1024]{1,0:T(8,128)(2,1)S(1)}, bf16[64,1024]{1,0:T(8,128)(2,1)}, u32[]{:S(2)}) copy-start(bf16[64,1024]{1,0:T(8,128)(2,1)} %param.13) | copy-start | bytes 393220
  7.2 122.0 %copy-start.1 = (bf16[64,1024]{1,0:T(8,128)(2,1)S(1)}, bf16[64,1024]{1,0:T(8,128)(2,1)}, u32[]{:S(2)}) copy-start(bf16[64,1024]{1,0:T(8,128)(2,1)} %param.11) | copy-start | bytes 393220
  7.2 122.0 %reduce-scatter.3.cloned.1.call-start = ((), (), s32[]{:S(2)}) async-start(), calls=%async_computation.2 | async-start | bytes 4456448 | tf_op jit(solution)/shard_map/reduce_scatter | solution.py:23
  31.1 161.4 %all-gather.3.cloned.1.call-start = ((), (), s32[]{:S(2)}) async-start(), calls=%async_computation.3 | async-start | bytes 2228224 | tf_op jit(solution)/shard_map/all_gather | solution.py:33
  131.0 123.5 %all-gather.5.cloned.1.call-start = ((), (), s32[]{:S(2)}) async-start(), calls=%async_computation.4 | async-start | bytes 2228224 | tf_op jit(solution)/shard_map/all_gather | solution.py:34
  131.7 200.8 %reduce-scatter.5.cloned.1.call-start = ((), (), s32[]{:S(2)}) async-start(), calls=%async_computation.5 | async-start | bytes 50331648 | tf_op jit(solution)/shard_map/reduce_scatter | solution.py:37
Sparse Core Ops, SparseCore 0:
  31.2 97.9 reduce-scatter.2
  132.6 59.8 all-gather.2
  195.3 59.1 all-gather.4
  291.2 41.2 reduce-scatter.4
where the time goes:
time: 348 us
  waiting for transfers between devices  235 us (68%)
  matrix products  87.8 us (25%)
  between operations  13.8 us (4%)
  other arithmetic  10.7 us (3%)
    reduce_scatter x1, waiting for transfers between devices, local(): lax.psum_scatter(lax.dot_general(integrals, multipliers, (((0,), (1,)), (...  98 us
    all_gather x1, waiting for transfers between devices, local(): lax.all_gather(renewed, 'vp', axis=0, tiled=True)  60.6 us
    reduce_scatter x1, waiting for transfers between devices, local(): lax.psum_scatter(first + jnp.dot(every_amp, multipliers, preferred_elemen...  41.4 us
    dot_general x1, matrix products, local(): jnp.dot(every_amp, multipliers, preferred_element_type=jnp.float32)  36.6 us
    all_gather x1, waiting for transfers between devices, local(): lax.all_gather(slab_amplitudes, 'vp', axis=0, tiled=True)  34.6 us
    dot_general x1, matrix products, local(): first = jnp.dot(every_new, amplitudes, preferred_element_type=jnp.float32)  27.4 us
    dot_general x1, matrix products, local(): lax.dot_general(integrals, multipliers, (((0,), (1,)), ((), ())), preferr...  23.8 us
    convert_element_type x1, other arithmetic, local(): return (renewed, density.astype(jnp.bfloat16))  8.92 us
  transfers between devices with their start and end apart: 4, of which 4 were waited for; matrix products, arithmetic and copies ran while one was open for 8% of the time, Pallas kernels for 0%

commit v1 on v0

v1 whole, which is shorter than its diff:
```python
import functools

import jax
import jax.numpy as jnp
from jax import lax
from jax.experimental import pallas as pl
from jax.experimental.pallas import tpu as pltpu
from jax.sharding import PartitionSpec as P


BF16, F32 = jnp.bfloat16, jnp.float32
LANES = 128
KERNEL_VMEM = 21 * 2**20


def divisor_at_most(extent, wanted):
    while extent % wanted:
        wanted //= 2
    return wanted


class Plan:
    def __init__(self, mesh, slab):
        self.n, self.cores = mesh.shape["vp"], mesh.shape["op"]
        self.bits = self.n.bit_length() - 1
        self.rows = slab // self.n
        top = self.bits - 1
        self.unit = LANES // self.rows
        low = self.unit.bit_length() - 1
        first, second = low, min(low + 1, top - 1)
        between = [b for b in range(self.bits) if b != top]
        up = [b for b in between if b != first]
        down = [b for b in reversed(between) if b != second]
        self.orders = ([first] + up + [top], [second] + down + [top])
        others = [b for b in between if b not in (first, second)]
        self.early = (
            others[:1] + [second, first] + others[1:] + [top],
            [first, second] + others + [top],
        )

    def exchange(self, x, step, orders=None):
        pairs = []
        for v in range(self.n):
            for c in range(self.cores):
                peer = v ^ (1 << (orders or self.orders)[c % 2][step])
                pairs.append((v * self.cores + c, peer * self.cores + c))
        return lax.ppermute(x, ("vp", "op"), pairs)

    def swap(self, x):
        return lax.ppermute(x, "op", [(c, c ^ 1) for c in range(self.cores)])

    def bit_at(self, core, step, orders=None):
        first, second = (orders or self.orders)[:2]
        return jnp.where(core == 0, first[step], second[step])

    def slot(self, me, core, block, orders):
        slot = me & (self.n // 2 - 1)
        for s in range(self.bits - 1):
            away = (block >> (self.bits - 2 - s)) & 1
            slot = slot ^ (away << self.bit_at(core, s, orders))
        return slot


def in_hbm():
    return pl.BlockSpec(memory_space=pltpu.HBM)


def in_vmem():
    return pl.BlockSpec(memory_space=pltpu.VMEM)


def in_smem():
    return pl.BlockSpec(memory_space=pltpu.SMEM)


def held(x):
    return pltpu.with_memory_space_constraint(x, pltpu.VMEM)


def far(x):
    return pltpu.with_memory_space_constraint(x, pltpu.HBM)


def ladder_half(plan, place, multipliers, integrals, keep):
    pairs, depth = multipliers.shape
    slab = integrals.shape[1]
    blocks = slab // LANES // 2
    tile = divisor_at_most(depth, 1024)
    steps = depth // tile
    low = plan.unit.bit_length() - 1
    out_type = F32 if keep else BF16

    def which(i, me, core):
        shift = plan.bit_at(core, 0) - low
        own = (me >> (shift + low)) & 1
        bit = own if keep else 1 - own
        rest = i & ((1 << shift) - 1)
        return ((i >> shift) << (shift + 1)) | (bit << shift) | rest

    def kernel(place_ref, m_ref, i_ref, out_ref, *refs):
        me, core = place_ref[0], place_ref[1]
        if keep:
            m_held, (i_held, total, i_sems) = m_ref, refs
        else:
            m_held, i_held, total, i_sems, m_sems = refs

        def span(k):
            return pl.ds(pl.multiple_of(k * tile, tile), tile)

        def m_copy(k):
            return pltpu.make_async_copy(m_ref.at[:, span(k)], m_held.at[:, span(k)], m_sems.at[k])

        def i_copy(k, i):
            lanes = pl.ds(pl.multiple_of(which(i, me, core) * LANES, LANES), LANES)
            return pltpu.make_async_copy(
                i_ref.at[span(k), lanes],
                i_held.at[span(k), pl.ds(i * LANES, LANES)],
                i_sems.at[k, i],
            )

        for k in range(steps):
            for i in range(blocks):
                i_copy(k, i).start()
            if not keep:
                m_copy(k).start()

        def arrive(k):
            for i in range(blocks):
                i_copy(k, i).wait()
            if not keep:
                m_copy(k).wait()

        def part(k, columns):
            return jnp.dot(m_held[:, span(k)], i_held[span(k), columns], preferred_element_type=F32)

        every = pl.ds(0, blocks * LANES)
        arrive(0)
        total[...] = part(0, every)

        def body(k, carry):
            arrive(k)
            total[...] += part(k, every)
            return carry

        lax.fori_loop(1, steps - 1, body, 0)
        arrive(steps - 1)
        for i in range(blocks):
            lanes = pl.ds(i * LANES, LANES)
            block = (total[:, lanes] + part(steps - 1, lanes)).T
            for t in range(plan.unit):
                away = (which(i, me, core) * plan.unit + t) ^ me
                slot = 0
                for s in range(1, plan.bits):
                    stays = 1 - ((away >> plan.bit_at(core, s)) & 1)
                    slot = slot * 2 + stays
                out_ref[slot] = block[t * plan.rows : (t + 1) * plan.rows].astype(out_type)

    out_shape = [pltpu.VMEM((plan.n // 2, plan.rows, pairs), out_type)]
    scratch = [
        pltpu.VMEM((depth, slab // 2), BF16),
        pltpu.VMEM((pairs, slab // 2), F32),
        pltpu.SemaphoreType.DMA((steps, blocks)),
    ]
    if not keep:
        out_shape.append(pltpu.VMEM((pairs, depth), BF16))
        scratch.append(pltpu.SemaphoreType.DMA((steps,)))
    return pl.pallas_call(
        kernel,
        in_specs=[in_smem(), in_vmem() if keep else in_hbm(), in_hbm()],
        out_specs=[in_vmem()] * len(out_shape),
        out_shape=out_shape,
        scratch_shapes=scratch,
        compiler_params=pltpu.CompilerParams(vmem_limit_bytes=KERNEL_VMEM),
        cost_estimate=pl.CostEstimate(
            flops=pairs * depth * slab,
            bytes_accessed=2 * (pairs * depth + depth * slab // 2 + pairs * slab),
            transcendentals=0,
        ),
        name="ladder_keep" if keep else "ladder_send",
    )(place, (held if keep else far)(multipliers), far(integrals))


def amplitude_part(plan, place, rows, own, other, begin, end, total):
    height, depth = rows.shape
    width = own.shape[1]
    tile = divisor_at_most(width // 4, 1024)
    base, steps = int(width * begin) // tile, int(width * (end - begin)) // tile
    half = depth // 2
    blocks = height // plan.rows

    def kernel(place_ref, l_ref, a_ref, b_ref, *refs):
        o_ref, a_held, b_held, sems = refs[-4:]
        me, core = place_ref[0], place_ref[1]

        def span(j):
            return pl.ds(pl.multiple_of((base + j) * tile, tile), tile)

        def copies(j):
            at = lax.rem(j, 2)
            return (
                pltpu.make_async_copy(a_ref.at[:, span(j)], a_held.at[at], sems.at[0, at]),
                pltpu.make_async_copy(b_ref.at[:, span(j)], b_held.at[at], sems.at[1, at]),
            )

        for c in copies(0):
            c.start()

        def body(j, carry):
            at = lax.rem(j, 2)

            @pl.when(j + 1 < steps)
            def _():
                for c in copies(j + 1):
                    c.start()

            a_copy, b_copy = copies(j)
            a_copy.wait()
            out = jnp.dot(l_ref[:, :half], a_held[at], preferred_element_type=F32)
            b_copy.wait()
            out = out + jnp.dot(l_ref[:, half:], b_held[at], preferred_element_type=F32)
            for i in range(blocks):
                slot = plan.slot(me, core, i, plan.early)
                o_ref[slot, :, span(j)] = out[i * plan.rows : (i + 1) * plan.rows]
            return carry

        lax.fori_loop(0, steps, body, 0)

    given = [] if total is None else [held(total)]
    return pl.pallas_call(
        kernel,
        in_specs=[in_smem(), in_vmem(), in_hbm(), in_hbm()] + [in_vmem()] * len(given),
        out_specs=in_vmem(),
        out_shape=pltpu.VMEM((blocks, plan.rows, width), F32),
        scratch_shapes=[
            pltpu.VMEM((2, half, tile), BF16),
            pltpu.VMEM((2, half, tile), BF16),
            pltpu.SemaphoreType.DMA((2, 2)),
        ],
        input_output_aliases={4: 0} if given else {},
        compiler_params=pltpu.CompilerParams(vmem_limit_bytes=KERNEL_VMEM),
        cost_estimate=pl.CostEstimate(
            flops=2 * height * depth * steps * tile,
            bytes_accessed=(2 * depth + 4 * height) * steps * tile,
            transcendentals=0,
        ),
    )(place, held(rows), far(own), far(other), *given)


def density(plan, place, rows, own, other, total):
    height, depth = sum(r.shape[0] for r in rows), rows[0].shape[1]
    width = own.shape[1]
    tile = divisor_at_most(width, 1024)
    steps = width // tile
    half = depth // 2
    blocks = height // plan.rows
    depth_of_queue = 2

    def kernel(
        place_ref, first_ref, second_ref, a_ref, b_ref, t_ref, o_ref, l_ref, a_held, b_held, o_held, l_sems, in_sems, out_sems
    ):
        me, core = place_ref[0], place_ref[1]

        def span(j):
            return pl.ds(pl.multiple_of(j * tile, tile), tile)

        def copies(j):
            at = lax.rem(j, depth_of_queue)
            return (
                pltpu.make_async_copy(a_ref.at[:, span(j)], a_held.at[at], in_sems.at[0, at]),
                pltpu.make_async_copy(b_ref.at[:, span(j)], b_held.at[at], in_sems.at[1, at]),
            )

        def put(j):
            at = lax.rem(j, 2)
            return pltpu.make_async_copy(o_held.at[at], o_ref.at[:, :, span(j)], out_sems.at[at])

        for c in copies(0):
            c.start()
        cut = first_ref.shape[0]
        joins = (
            pltpu.make_async_copy(first_ref, l_ref.at[pl.ds(0, cut)], l_sems.at[0]),
            pltpu.make_async_copy(second_ref, l_ref.at[pl.ds(cut, height - cut)], l_sems.at[1]),
        )
        for c in joins:
            c.start()
        for c in joins:
            c.wait()

        def body(j, carry):
            at = lax.rem(j, depth_of_queue)

            @pl.when(j + 1 < steps)
            def _():
                for c in copies(j + 1):
                    c.start()

            @pl.when(j >= 2)
            def _():
                put(j - 2).wait()

            a_copy, b_copy = copies(j)
            a_copy.wait()
            out = jnp.dot(l_ref[:, :half], a_held[at], preferred_element_type=F32)
            b_copy.wait()
            out = out + jnp.dot(l_ref[:, half:], b_held[at], preferred_element_type=F32)
            for i in range(blocks):
                slot = plan.slot(me, core, i, plan.orders)
                new = t_ref[slot, :, span(j)] + out[i * plan.rows : (i + 1) * plan.rows]
                o_held[lax.rem(j, 2), slot] = new.astype(BF16)
            put(j).start()
            return carry

        lax.fori_loop(0, steps, body, 0)
        for j in range(max(steps - 2, 0), steps):
            put(j).wait()

    return pl.pallas_call(
        kernel,
        in_specs=[in_smem(), in_vmem(), in_vmem(), in_hbm(), in_hbm(), in_vmem()],
        out_specs=in_hbm(),
        out_shape=jax.ShapeDtypeStruct((blocks, plan.rows, width), BF16),
        scratch_shapes=[
            pltpu.VMEM((height, depth), BF16),
            pltpu.VMEM((depth_of_queue, half, tile), BF16),
            pltpu.VMEM((depth_of_queue, half, tile), BF16),
            pltpu.VMEM((2, blocks, plan.rows, tile), BF16),
            pltpu.SemaphoreType.DMA((2,)),
            pltpu.SemaphoreType.DMA((2, depth_of_queue)),
            pltpu.SemaphoreType.DMA((2,)),
        ],
        compiler_params=pltpu.CompilerParams(vmem_limit_bytes=KERNEL_VMEM),
        cost_estimate=pl.CostEstimate(
            flops=2 * height * depth * width,
            bytes_accessed=2 * depth * width + 2 * height * width,
            transcendentals=0,
        ),
        name="density",
    )(place, *map(held, rows), far(own), far(other), held(total)).reshape(height, width)


def renew_slab(current, ladder, rest, virtual, occupied):
    divisor = virtual.astype(F32)[:, None] - occupied.astype(F32)[None, :]
    renewed = current.astype(F32) + (ladder + rest.astype(F32)) / divisor
    return renewed.astype(BF16)


def split(total):
    half = total.shape[0] // 2
    return total[:half].astype(BF16), total[half:]


def both_cores(plan, here, mine, across):
    stays = jnp.where(here > 0, mine, across)
    leaves = jnp.where(here > 0, across, mine)
    return jnp.concatenate([stays, plan.swap(leaves)], axis=1)


def local(
    plan,
    multipliers,
    integrals,
    amplitudes,
    slab_multipliers,
    slab_amplitudes,
    residual_rest,
    occupied_energy,
    virtual_energy,
):
    after = lax.optimization_barrier
    last = plan.bits - 1
    me, core = lax.axis_index("vp"), lax.axis_index("op")
    here = jnp.full(slab_amplitudes.shape, core == me // (plan.n // 2), F32)
    place, here = after((jnp.stack([me, core]).astype(jnp.int32), here))
    across = plan.exchange(slab_amplitudes, last)
    sent, in_reach = ladder_half(plan, place, multipliers, integrals, keep=False)
    later, across, sent = after((place, across, sent))
    arrived = plan.exchange(sent, 0)
    amp = both_cores(plan, here, slab_amplitudes, across)
    amp, to_swap = after((amp, in_reach))
    their_multipliers = plan.swap(to_swap)
    amp_next = plan.exchange(amp, last - 1, plan.early)
    (kept,) = ladder_half(plan, later, in_reach, integrals, keep=True)
    kept, amp_next, to_swap = after((kept, amp_next, amplitudes))
    their_amplitudes = plan.swap(to_swap)
    amp = jnp.concatenate([amp, amp_next], axis=0)
    waiting = list(range(last - 2, -1, -1))
    for step in range(1, plan.bits):
        sent, kept = split(kept + arrived.astype(F32))
        if step > 1 and len(waiting) > 1:
            amp_next = plan.exchange(amp, waiting.pop(0), plan.early)
            amp = jnp.concatenate([amp, amp_next], axis=0)
            sent, amp = after((sent, amp))
        arrived = plan.exchange(sent, step)
    for step in waiting:
        amp = jnp.concatenate([amp, plan.exchange(amp, step, plan.early)], axis=0)
    ladder = (kept + arrived.astype(F32)).reshape(kept.shape[-2:])
    renewed = renew_slab(slab_multipliers, ladder, residual_rest, virtual_energy, occupied_energy)

    part = functools.partial(amplitude_part, plan, place, amp, multipliers, their_multipliers)
    across = plan.exchange(renewed, last)
    across, total = after((across, part(0, 0.25, None)))
    rows = both_cores(plan, here, renewed, across)
    for step in range(last - 1, -1, -1):
        rows_next = plan.exchange(rows, step)
        if step == 1:
            rows_next, total, their_amplitudes = after((rows_next, part(0.25, 0.5, total), their_amplitudes))
        if step == 0:
            rows_next, total = after((rows_next, part(0.5, 1.0, total)))
            break
        rows = jnp.concatenate([rows, rows_next], axis=0)
    return renewed, density(plan, place, (rows, rows_next), amplitudes, their_amplitudes, total)


def solution(mesh):
    def whole(*args):
        plan = Plan(mesh, args[1].shape[1])

        def body(*blocks):
            return local(plan, *blocks)

        return jax.shard_map(
            body,
            mesh=mesh,
            in_specs=(
                P("op", "vp"),
                P("vp", None),
                P("op", "vp"),
                P("vp", "op"),
                P("vp", "op"),
                P("vp", "op"),
                P("op"),
                P("vp"),
            ),
            out_specs=(P("vp", "op"), P("op", "vp")),
            check_vma=False,
        )(*args)

    return whole
```

time: 348 us -> 150 us (0.43)
  waiting for transfers between devices: 235 us -> 42 us
  matrix products: 87.8 us -> 0 us
  Pallas kernels: 0 us -> 82.4 us
  starting transfers between devices: 0.34 us -> 22.2 us
  between operations: 13.8 us -> 1.16 us
  other arithmetic: 10.7 us -> 1.27 us
    reduce_scatter x2 -> x0, waiting for transfers between devices: 139 us -> none  [the longest x1 98 us: local(): lax.psum_scatter(lax.dot_general(integrals, multipliers, (((0,), (1,)), (...]
    all_gather x2 -> x0, waiting for transfers between devices: 95.1 us -> none  [the longest x1 60.6 us: local(): lax.all_gather(renewed, 'vp', axis=0, tiled=True)]
    dot_general x3 -> x0, matrix products: 87.8 us -> none  [the longest x1 36.6 us: local(): jnp.dot(every_amp, multipliers, preferred_element_type=jnp.float32)]
    pallas_call x0 -> x6, Pallas kernels: none -> 82.4 us  [the longest x2 30 us: ladder_half(): pl.pallas_call(kernel, in_specs=[in_smem(), in_vmem() if keep else in_hbm...]
    ppermute x0 -> x16, waiting for transfers between devices: none -> 42 us  [the longest x12 39.6 us: exchange(): return lax.ppermute(x, ('vp', 'op'), pairs)]
    ppermute x0 -> x16, starting transfers between devices: none -> 22.2 us  [the longest x12 17.3 us: exchange(): return lax.ppermute(x, ('vp', 'op'), pairs)]
    convert_element_type x4 -> x3, other arithmetic: 10.7 us -> 0.13 us  [the longest x1 0.13 us: renew_slab(): return renewed.astype(BF16)]
  transfers between devices with their start and end apart: 4 -> 16, of which waited for: 4 -> 10; matrix products, arithmetic and copies ran while one was open for 8% -> 1% of each run, Pallas kernels for 0% -> 39%
where the time goes in v1:
time: 150 us; the launch traced here: 149 us
  Pallas kernels  82.4 us (55%)
  waiting for transfers between devices  42 us (28%)
  starting transfers between devices  22.2 us (15%)
    ppermute x12, waiting for transfers between devices, exchange(): return lax.ppermute(x, ('vp', 'op'), pairs)  39.6 us
    pallas_call x2, Pallas kernels, ladder_half(): pl.pallas_call(kernel, in_specs=[in_smem(), in_vmem() if keep else in_hbm...  30 us
    pallas_call x3, Pallas kernels, amplitude_part(): pl.pallas_call(kernel, in_specs=[in_smem(), in_vmem(), in_hbm(), in_hbm()...  28.2 us
    pallas_call x1, Pallas kernels, density(): pl.pallas_call(kernel, in_specs=[in_smem(), in_vmem(), in_vmem(), in_hbm(...  24.3 us
    ppermute x12, starting transfers between devices, exchange(): return lax.ppermute(x, ('vp', 'op'), pairs)  17.3 us
    ppermute x4, starting transfers between devices, swap(): return lax.ppermute(x, 'op', [(c, c ^ 1) for c in range(self.cores)])  4.92 us
  transfers between devices with their start and end apart: 16, of which 10 were waited for; matrix products, arithmetic and copies ran while one was open for 1% of the time, Pallas kernels for 39%

profile of v1, /device:TPU:0, one launch (start us, length us, event | category | flops | bytes accessed | tf_op | source)
XLA Modules:
  0.0 149.4 jit_solution(17353054059744825771)
XLA Ops:
  0.6 4.1 %collective-permute-start = (bf16[64,1024]{1,0:T(8,128)(2,1)}, bf16[64,1024]{1,0:T(8,128)(2,1)S(1)}, u32[]{:S(2)}, u32[]{:S(2)}) collective-permute-start(bf16[64,1024]{1,0:T(8,128)(2,1)} %param.12), channel_id=1, source_target_pairs={{0,16},{1,17},{2,18},{3,19},{4,20},{5,21},{6,22},{7,23},{8,24},{9,... | collective-permute-start | bytes 393224 | tf_op jit(solution)/shard_map/ppermute | solution.py:47
  4.9 15.9 %ladder_send.1 = (bf16[8,64,1024]{2,1,0:T(8,128)(2,1)S(1)}, bf16[1024,8192]{1,0:T(8,128)(2,1)S(1)}) custom-call(s32[2]{0:T(128)S(1)} %pad_add_fusion.place_ref, bf16[1024,8192]{1,0:T(8,128)(2,1)} %a_ref.6, bf16[8192,1024]{1,0:T(8,128)(2,1)} %i_ref.3), custom_call_target="tpu_custom_call" | custom-call | flops 8589934592 | bytes 27262976 | tf_op jit(solution)/shard_map/ladder_send/pallas_call | solution.py:167
  21.0 1.3 collective-permute-done.1
  22.4 0.2 collective-permute-start.10
  22.6 1.5 %collective-permute-start.2 = (bf16[64,2048]{1,0:T(8,128)(2,1)S(1)}, bf16[64,2048]{1,0:T(8,128)(2,1)S(1)}, u32[]{:S(2)}, u32[]{:S(2)}) collective-permute-start(bf16[64,2048]{1,0:T(8,128)(2,1)S(1)} %pad_maximum_fusion.4), channel_id=1, source_target_pairs={{0,4},{1,3},{2,6},{3,1},{4,0},{5,7},{6,2},{7,5},{8,12},{9,11},{10,... | collective-permute-start | bytes 786440 | tf_op jit(solution)/shard_map/ppermute | solution.py:47
  24.1 14.1 %ladder_keep.1 = f32[8,64,1024]{2,1,0:T(8,128)S(1)} custom-call(s32[2]{0:T(128)S(1)} %pad_add_fusion.place_ref, bf16[1024,8192]{1,0:T(8,128)(2,1)S(1)} %get-tuple-element.35.m_ref, bf16[8192,1024]{1,0:T(8,128)(2,1)} %i_ref.3), custom_call_target="tpu_custom_call" | custom-call | flops 8589934592 | bytes 27262976 | tf_op jit(solution)/shard_map/ladder_keep/pallas_call | solution.py:167
  38.3 0.1 collective-permute-start.14
  38.4 1.5 %collective-permute-start.3 = (bf16[8,64,1024]{2,1,0:T(8,128)(2,1)S(1)}, bf16[8,64,1024]{2,1,0:T(8,128)(2,1)S(1)}, u32[]{:S(2)}, u32[]{:S(2)}) collective-permute-start(bf16[8,64,1024]{2,1,0:T(8,128)(2,1)S(1)} %get-tuple-element.31), channel_id=1, source_target_pairs={{0,4},{1,9},{2,6},{3,11},{4,0},{5,13},{6,2},{7,15},{8,12},{9,1},{1... | collective-permute-start | bytes 3145736 | tf_op jit(solution)/shard_map/ppermute | solution.py:47
  40.0 1.6 %collective-permute-start.5 = (bf16[128,2048]{1,0:T(8,128)(2,1)S(1)}, bf16[128,2048]{1,0:T(8,128)(2,1)S(1)}, u32[]{:S(2)}, u32[]{:S(2)}) collective-permute-start(bf16[128,2048]{1,0:T(8,128)(2,1)S(1)} %pad_maximum_fusion.2), channel_id=1, source_target_pairs={{0,8},{1,9},{2,10},{3,11},{4,12},{5,13},{6,14},{7,15},{8,0},{9,1},... | collective-permute-start | bytes 1572872 | tf_op jit(solution)/shard_map/ppermute | solution.py:47
  41.6 11.6 %collective-permute-done.3 = bf16[8,64,1024]{2,1,0:T(8,128)(2,1)S(1)} collective-permute-done((bf16[8,64,1024]{2,1,0:T(8,128)(2,1)S(1)}, bf16[8,64,1024]{2,1,0:T(8,128)(2,1)S(1)}, u32[]{:S(2)}, u32[]{:S(2)}) %collective-permute-start.3) | collective-permute-done | bytes 1048608 | tf_op jit(solution)/shard_map/ppermute | solution.py:47
  53.2 0.4 convert_add_fusion
  53.8 1.6 %collective-permute-start.4 = (bf16[4,64,1024]{2,1,0:T(8,128)(2,1)S(1)}, bf16[4,64,1024]{2,1,0:T(8,128)(2,1)S(1)}, u32[]{:S(2)}, u32[]{:S(2)}) collective-permute-start(bf16[4,64,1024]{2,1,0:T(8,128)(2,1)S(1)} %slice.49), channel_id=1, source_target_pairs={{0,2},{1,5},{2,0},{3,7},{4,6},{5,1},{6,4},{7,3},{8,10},{9,13},{10,... | collective-permute-start | bytes 1572872 | tf_op jit(solution)/shard_map/ppermute | solution.py:47
  55.4 7.6 %collective-permute-done.4 = bf16[4,64,1024]{2,1,0:T(8,128)(2,1)S(1)} collective-permute-done((bf16[4,64,1024]{2,1,0:T(8,128)(2,1)S(1)}, bf16[4,64,1024]{2,1,0:T(8,128)(2,1)S(1)}, u32[]{:S(2)}, u32[]{:S(2)}) %collective-permute-start.4) | collective-permute-done | bytes 524320 | tf_op jit(solution)/shard_map/ppermute | solution.py:47
  63.0 0.1 slice_add_fusion
  63.2 1.6 %collective-permute-start.9 = (bf16[256,2048]{1,0:T(8,128)(2,1)S(1)}, bf16[256,2048]{1,0:T(8,128)(2,1)S(1)}, u32[]{:S(2)}, u32[]{:S(2)}) collective-permute-start(bf16[256,2048]{1,0:T(8,128)(2,1)S(1)} %pad_maximum_fusion), channel_id=1, source_target_pairs={{0,2},{1,5},{2,0},{3,7},{4,6},{5,1},{6,4},{7,3},{8,10},{9,13},{10,... | collective-permute-start | bytes 3145736 | tf_op jit(solution)/shard_map/ppermute | solution.py:47
  64.8 1.6 %collective-permute-start.6 = (bf16[2,64,1024]{2,1,0:T(8,128)(2,1)S(1)}, bf16[2,64,1024]{2,1,0:T(8,128)(2,1)S(1)}, u32[]{:S(2)}, u32[]{:S(2)}) collective-permute-start(bf16[2,64,1024]{2,1,0:T(8,128)(2,1)S(1)} %slice.50), channel_id=1, source_target_pairs={{0,8},{1,3},{2,10},{3,1},{4,12},{5,7},{6,14},{7,5},{8,0},{9,11},{1... | collective-permute-start | bytes 786440 | tf_op jit(solution)/shard_map/ppermute | solution.py:47
  66.4 4.8 %collective-permute-done.6 = bf16[2,64,1024]{2,1,0:T(8,128)(2,1)S(1)} collective-permute-done((bf16[2,64,1024]{2,1,0:T(8,128)(2,1)S(1)}, bf16[2,64,1024]{2,1,0:T(8,128)(2,1)S(1)}, u32[]{:S(2)}, u32[]{:S(2)}) %collective-permute-start.6) | collective-permute-done | bytes 262176 | tf_op jit(solution)/shard_map/ppermute | solution.py:47
  71.2 0.4 collective-permute-start.7
  71.7 6.8 %collective-permute-done.7 = bf16[1,64,1024]{2,1,0:T(8,128)(2,1)S(1)} collective-permute-done((bf16[1,64,1024]{2,1,0:T(8,128)(2,1)S(1)}, bf16[1,64,1024]{2,1,0:T(8,128)(2,1)S(1)}, u32[]{:S(2)}, u32[]{:S(2)}) %collective-permute-start.7) | collective-permute-done | bytes 131104 | tf_op jit(solution)/shard_map/ppermute | solution.py:47
  78.8 2.1 %collective-permute-done.9 = bf16[256,2048]{1,0:T(8,128)(2,1)S(1)} collective-permute-done((bf16[256,2048]{1,0:T(8,128)(2,1)S(1)}, bf16[256,2048]{1,0:T(8,128)(2,1)S(1)}, u32[]{:S(2)}, u32[]{:S(2)}) %collective-permute-start.9) | collective-permute-done | bytes 1048608 | tf_op jit(solution)/shard_map/ppermute | solution.py:47
  81.0 7.7 %shard_map.95.refs_0_ = f32[8,64,8192]{2,1,0:T(8,128)S(1)} custom-call(s32[2]{0:T(128)S(1)} %pad_add_fusion.place_ref, bf16[512,2048]{1,0:T(8,128)(2,1)S(1)} %constant_dynamic-update-slice_fusion.l_ref, bf16[1024,8192]{1,0:T(8,128)(2,1)} %a_ref.6, bf16[1024,8192]{1,0:T(8,128)(2,1)} %collective-permute-done.10.b_ref), custom_call_target="tpu_custom_call" | custom-call | flops 4294967296 | bytes 12582912 | tf_op jit(solution)/shard_map/pallas_call | solution.py:229
  88.7 4.5 %collective-permute-start.11 = (bf16[64,1024]{1,0:T(8,128)(2,1)S(1)}, bf16[64,1024]{1,0:T(8,128)(2,1)S(1)}, u32[]{:S(2)}, u32[]{:S(2)}) collective-permute-start(bf16[64,1024]{1,0:T(8,128)(2,1)S(1)} %get-tuple-element.47), channel_id=1, source_target_pairs={{0,1},{1,0},{2,3},{3,2},{4,5},{5,4},{6,7},{7,6},{8,9},{9,8},{10,11... | collective-permute-start | bytes 393224 | tf_op jit(solution)/shard_map/ppermute | solution.py:50
  93.2 1.0 collective-permute-done.11
  94.2 1.5 %collective-permute-start.12 = (bf16[64,2048]{1,0:T(8,128)(2,1)S(1)}, bf16[64,2048]{1,0:T(8,128)(2,1)S(1)}, u32[]{:S(2)}, u32[]{:S(2)}) collective-permute-start(bf16[64,2048]{1,0:T(8,128)(2,1)S(1)} %pad_maximum_fusion.5), channel_id=1, source_target_pairs={{0,8},{1,3},{2,10},{3,1},{4,12},{5,7},{6,14},{7,5},{8,0},{9,11},{1... | collective-permute-start | bytes 786440 | tf_op jit(solution)/shard_map/ppermute | solution.py:47
  95.7 4.9 %collective-permute-done.12 = bf16[64,2048]{1,0:T(8,128)(2,1)S(1)} collective-permute-done((bf16[64,2048]{1,0:T(8,128)(2,1)S(1)}, bf16[64,2048]{1,0:T(8,128)(2,1)S(1)}, u32[]{:S(2)}, u32[]{:S(2)}) %collective-permute-start.12) | collective-permute-done | bytes 262176 | tf_op jit(solution)/shard_map/ppermute | solution.py:47
  100.7 0.8 collective-permute-start.13
  101.5 7.7 %shard_map.96.refs_0_ = f32[8,64,8192]{2,1,0:T(8,128)S(1)} custom-call(s32[2]{0:T(128)S(1)} %pad_add_fusion.place_ref, bf16[512,2048]{1,0:T(8,128)(2,1)S(1)} %constant_dynamic-update-slice_fusion.l_ref, bf16[1024,8192]{1,0:T(8,128)(2,1)} %a_ref.6, bf16[1024,8192]{1,0:T(8,128)(2,1)} %collective-permute-done.10.b_ref, ...), custom_call_target="tpu_custom_call", output_to_operand_aliasing={{}: (4, {})} | custom-call | flops 4294967296 | bytes 12582912 | tf_op jit(solution)/shard_map/pallas_call | solution.py:229
  109.2 0.8 collective-permute-done.13
  110.1 1.0 collective-permute-start.15
  111.1 12.8 %shard_map.97.t_ref = f32[8,64,8192]{2,1,0:T(8,128)S(1)} custom-call(s32[2]{0:T(128)S(1)} %pad_add_fusion.place_ref, bf16[512,2048]{1,0:T(8,128)(2,1)S(1)} %constant_dynamic-update-slice_fusion.l_ref, bf16[1024,8192]{1,0:T(8,128)(2,1)} %a_ref.6, bf16[1024,8192]{1,0:T(8,128)(2,1)} %collective-permute-done.10.b_ref, ...), custom_call_target="tpu_custom_call", output_to_operand_aliasing={{}: (4, {})} | custom-call | flops 8589934592 | bytes 25165824 | tf_op jit(solution)/shard_map/pallas_call | solution.py:229
  123.9 1.0 collective-permute-done.15.second_ref
  124.9 24.3 %density.1 = bf16[8,64,8192]{2,1,0:T(8,128)(2,1)} custom-call(s32[2]{0:T(128)S(1)} %pad_add_fusion.place_ref, bf16[256,2048]{1,0:T(8,128)(2,1)S(1)} %pad_maximum_fusion.1.first_ref, bf16[256,2048]{1,0:T(8,128)(2,1)S(1)} %collective-permute-done.15.second_ref, bf16[1024,8192]{1,0:T(8,128)(2,1)} %a_ref.7, bf16[1024,8192]{1,0:T(8,128)(2,1)} %collective-permute-done.14.b_ref, ...), custom_call_target="tpu_custom_call" | custom-call | flops 17179869184 | bytes 41943040 | tf_op jit(solution)/shard_map/density/pallas_call | solution.py:317
  (49 shorter events, 1.2 us)
Async XLA Ops:
  0.6 20.1 %collective-permute-start = (bf16[64,1024]{1,0:T(8,128)(2,1)}, bf16[64,1024]{1,0:T(8,128)(2,1)S(1)}, u32[]{:S(2)}, u32[]{:S(2)}) collective-permute-start(bf16[64,1024]{1,0:T(8,128)(2,1)} %param.12), channel_id=1, source_target_pairs={{0,16},{1,17},{2,18},{3,19},{4,20},{5,21},{6,22},{7,23},{8,24},{9,... | collective-permute-start | bytes 393224 | tf_op jit(solution)/shard_map/ppermute | solution.py:47
  4.9 15.9 %copy-start = (bf16[64,1024]{1,0:T(8,128)(2,1)S(1)}, bf16[64,1024]{1,0:T(8,128)(2,1)}, u32[]{:S(2)}) copy-start(bf16[64,1024]{1,0:T(8,128)(2,1)} %param.12) | copy-start | bytes 393220
  20.9 1.4 collective-permute-start.1
  22.4 15.9 %slice-start = ((s8[16777216]{0:T(1024)(128)(4,1)}), s8[4194304]{0:T(1024)(128)(4,1)S(1)}, s32[]{:S(2)}) async-start(s8[16777216]{0:T(1024)(128)(4,1)} %bitcast.13), calls=%async_computation | async-start | bytes 8388608
  22.4 15.9 %slice-start.1 = ((s8[16777216]{0:T(1024)(128)(4,1)}), s8[4194304]{0:T(1024)(128)(4,1)S(1)}, s32[]{:S(2)}) async-start(s8[16777216]{0:T(1024)(128)(4,1)} %bitcast.13), calls=%async_computation.1 | async-start | bytes 8388608
  22.4 15.9 %slice-start.2 = ((s8[16777216]{0:T(1024)(128)(4,1)}), s8[4194304]{0:T(1024)(128)(4,1)S(1)}, s32[]{:S(2)}) async-start(s8[16777216]{0:T(1024)(128)(4,1)} %bitcast.13), calls=%async_computation.2 | async-start | bytes 8388608
  22.4 15.9 %slice-start.3 = ((s8[16777216]{0:T(1024)(128)(4,1)}), s8[4194304]{0:T(1024)(128)(4,1)S(1)}, s32[]{:S(2)}) async-start(s8[16777216]{0:T(1024)(128)(4,1)} %bitcast.13), calls=%async_computation.3 | async-start | bytes 8388608
  22.4 58.5 %collective-permute-start.10 = (bf16[1024,8192]{1,0:T(8,128)(2,1)S(1)}, bf16[1024,8192]{1,0:T(8,128)(2,1)}, u32[]{:S(2)}, u32[]{:S(2)}) collective-permute-start(bf16[1024,8192]{1,0:T(8,128)(2,1)S(1)} %get-tuple-element.35.m_ref), channel_id=1, source_target_pairs={{0,1},{1,0},{2,3},{3,2},{4,5},{5,4},{6,7},{7,6},{8,9},{9,8},{10,11... | collective-permute-start | bytes 50331656 | tf_op jit(solution)/shard_map/ppermute | solution.py:50
  22.6 15.6 %collective-permute-start.2 = (bf16[64,2048]{1,0:T(8,128)(2,1)S(1)}, bf16[64,2048]{1,0:T(8,128)(2,1)S(1)}, u32[]{:S(2)}, u32[]{:S(2)}) collective-permute-start(bf16[64,2048]{1,0:T(8,128)(2,1)S(1)} %pad_maximum_fusion.4), channel_id=1, source_target_pairs={{0,4},{1,3},{2,6},{3,1},{4,0},{5,7},{6,2},{7,5},{8,12},{9,11},{10,... | collective-permute-start | bytes 786440 | tf_op jit(solution)/shard_map/ppermute | solution.py:47
  38.3 70.9 %collective-permute-start.14 = (bf16[1024,8192]{1,0:T(8,128)(2,1)S(1)}, bf16[1024,8192]{1,0:T(8,128)(2,1)}, u32[]{:S(2)}, u32[]{:S(2)}) collective-permute-start(bf16[1024,8192]{1,0:T(8,128)(2,1)S(1)} %bitcast.14), channel_id=1, source_target_pairs={{0,1},{1,0},{2,3},{3,2},{4,5},{5,4},{6,7},{7,6},{8,9},{9,8},{10,11... | collective-permute-start | bytes 50331656 | tf_op jit(solution)/shard_map/ppermute | solution.py:50
  38.4 14.8 %collective-permute-start.3 = (bf16[8,64,1024]{2,1,0:T(8,128)(2,1)S(1)}, bf16[8,64,1024]{2,1,0:T(8,128)(2,1)S(1)}, u32[]{:S(2)}, u32[]{:S(2)}) collective-permute-start(bf16[8,64,1024]{2,1,0:T(8,128)(2,1)S(1)} %get-tuple-element.31), channel_id=1, source_target_pairs={{0,4},{1,9},{2,6},{3,11},{4,0},{5,13},{6,2},{7,15},{8,12},{9,1},{1... | collective-permute-start | bytes 3145736 | tf_op jit(solution)/shard_map/ppermute | solution.py:47
  40.0 15.3 %collective-permute-start.5 = (bf16[128,2048]{1,0:T(8,128)(2,1)S(1)}, bf16[128,2048]{1,0:T(8,128)(2,1)S(1)}, u32[]{:S(2)}, u32[]{:S(2)}) collective-permute-start(bf16[128,2048]{1,0:T(8,128)(2,1)S(1)} %pad_maximum_fusion.2), channel_id=1, source_target_pairs={{0,8},{1,9},{2,10},{3,11},{4,12},{5,13},{6,14},{7,15},{8,0},{9,1},... | collective-permute-start | bytes 1572872 | tf_op jit(solution)/shard_map/ppermute | solution.py:47
  53.8 9.2 %collective-permute-start.4 = (bf16[4,64,1024]{2,1,0:T(8,128)(2,1)S(1)}, bf16[4,64,1024]{2,1,0:T(8,128)(2,1)S(1)}, u32[]{:S(2)}, u32[]{:S(2)}) collective-permute-start(bf16[4,64,1024]{2,1,0:T(8,128)(2,1)S(1)} %slice.49), channel_id=1, source_target_pairs={{0,2},{1,5},{2,0},{3,7},{4,6},{5,1},{6,4},{7,3},{8,10},{9,13},{10,... | collective-permute-start | bytes 1572872 | tf_op jit(solution)/shard_map/ppermute | solution.py:47
  55.4 10.9 %copy-start.5 = (bf16[64]{0:T(256)(128)(2,1)S(1)}, bf16[64]{0:T(256)(128)(2,1)}, u32[]{:S(2)}) copy-start(bf16[64]{0:T(256)(128)(2,1)} %param.15) | copy-start | bytes 388
  55.4 10.9 %copy-start.4 = (bf16[1024]{0:T(1024)(128)(2,1)S(1)}, bf16[1024]{0:T(1024)(128)(2,1)}, u32[]{:S(2)}) copy-start(bf16[1024]{0:T(1024)(128)(2,1)} %param.14) | copy-start | bytes 6148
  63.1 15.4 %copy-start.2 = (bf16[64,1024]{1,0:T(8,128)(2,1)S(1)}, bf16[64,1024]{1,0:T(8,128)(2,1)}, u32[]{:S(2)}) copy-start(bf16[64,1024]{1,0:T(8,128)(2,1)} %param.13) | copy-start | bytes 393220
  63.2 15.4 %copy-start.3 = (bf16[64,1024]{1,0:T(8,128)(2,1)S(1)}, bf16[64,1024]{1,0:T(8,128)(2,1)}, u32[]{:S(2)}) copy-start(bf16[64,1024]{1,0:T(8,128)(2,1)} %param.11) | copy-start | bytes 393220
  63.2 17.7 %collective-permute-start.9 = (bf16[256,2048]{1,0:T(8,128)(2,1)S(1)}, bf16[256,2048]{1,0:T(8,128)(2,1)S(1)}, u32[]{:S(2)}, u32[]{:S(2)}) collective-permute-start(bf16[256,2048]{1,0:T(8,128)(2,1)S(1)} %pad_maximum_fusion), channel_id=1, source_target_pairs={{0,2},{1,5},{2,0},{3,7},{4,6},{5,1},{6,4},{7,3},{8,10},{9,13},{10,... | collective-permute-start | bytes 3145736 | tf_op jit(solution)/shard_map/ppermute | solution.py:47
  64.8 6.4 %collective-permute-start.6 = (bf16[2,64,1024]{2,1,0:T(8,128)(2,1)S(1)}, bf16[2,64,1024]{2,1,0:T(8,128)(2,1)S(1)}, u32[]{:S(2)}, u32[]{:S(2)}) collective-permute-start(bf16[2,64,1024]{2,1,0:T(8,128)(2,1)S(1)} %slice.50), channel_id=1, source_target_pairs={{0,8},{1,3},{2,10},{3,1},{4,12},{5,7},{6,14},{7,5},{8,0},{9,11},{1... | collective-permute-start | bytes 786440 | tf_op jit(solution)/shard_map/ppermute | solution.py:47
  71.2 7.3 %collective-permute-start.7 = (bf16[1,64,1024]{2,1,0:T(8,128)(2,1)S(1)}, bf16[1,64,1024]{2,1,0:T(8,128)(2,1)S(1)}, u32[]{:S(2)}, u32[]{:S(2)}) collective-permute-start(bf16[1,64,1024]{2,1,0:T(8,128)(2,1)S(1)} %slice.51), channel_id=1, source_target_pairs={{0,16},{1,17},{2,18},{3,19},{4,20},{5,21},{6,22},{7,23},{8,24},{9,... | collective-permute-start | bytes 393224 | tf_op jit(solution)/shard_map/ppermute | solution.py:47
  78.7 10.0 %copy-start.1 = (bf16[64,1024]{1,0:T(8,128)(2,1)}, bf16[64,1024]{1,0:T(8,128)(2,1)S(1)}, u32[]{:S(2)}) copy-start(bf16[64,1024]{1,0:T(8,128)(2,1)S(1)} %fusion.4) | copy-start | bytes 393220
  78.7 9.9 %collective-permute-start.8 = (bf16[64,1024]{1,0:T(8,128)(2,1)S(1)}, bf16[64,1024]{1,0:T(8,128)(2,1)S(1)}, u32[]{:S(2)}, u32[]{:S(2)}) collective-permute-start(bf16[64,1024]{1,0:T(8,128)(2,1)S(1)} %fusion.4), channel_id=1, source_target_pairs={{0,16},{1,17},{2,18},{3,19},{4,20},{5,21},{6,22},{7,23},{8,24},{9,... | collective-permute-start | bytes 393224 | tf_op jit(solution)/shard_map/ppermute | solution.py:47
  88.7 5.5 %collective-permute-start.11 = (bf16[64,1024]{1,0:T(8,128)(2,1)S(1)}, bf16[64,1024]{1,0:T(8,128)(2,1)S(1)}, u32[]{:S(2)}, u32[]{:S(2)}) collective-permute-start(bf16[64,1024]{1,0:T(8,128)(2,1)S(1)} %get-tuple-element.47), channel_id=1, source_target_pairs={{0,1},{1,0},{2,3},{3,2},{4,5},{5,4},{6,7},{7,6},{8,9},{9,8},{10,11... | collective-permute-start | bytes 393224 | tf_op jit(solution)/shard_map/ppermute | solution.py:50
  94.2 6.4 %collective-permute-start.12 = (bf16[64,2048]{1,0:T(8,128)(2,1)S(1)}, bf16[64,2048]{1,0:T(8,128)(2,1)S(1)}, u32[]{:S(2)}, u32[]{:S(2)}) collective-permute-start(bf16[64,2048]{1,0:T(8,128)(2,1)S(1)} %pad_maximum_fusion.5), channel_id=1, source_target_pairs={{0,8},{1,3},{2,10},{3,1},{4,12},{5,7},{6,14},{7,5},{8,0},{9,11},{1... | collective-permute-start | bytes 786440 | tf_op jit(solution)/shard_map/ppermute | solution.py:47
  100.7 9.2 %collective-permute-start.13 = (bf16[128,2048]{1,0:T(8,128)(2,1)S(1)}, bf16[128,2048]{1,0:T(8,128)(2,1)S(1)}, u32[]{:S(2)}, u32[]{:S(2)}) collective-permute-start(bf16[128,2048]{1,0:T(8,128)(2,1)S(1)} %pad_maximum_fusion.3), channel_id=1, source_target_pairs={{0,2},{1,5},{2,0},{3,7},{4,6},{5,1},{6,4},{7,3},{8,10},{9,13},{10,... | collective-permute-start | bytes 1572872 | tf_op jit(solution)/shard_map/ppermute | solution.py:47
  110.1 14.9 %collective-permute-start.15 = (bf16[256,2048]{1,0:T(8,128)(2,1)S(1)}, bf16[256,2048]{1,0:T(8,128)(2,1)S(1)}, u32[]{:S(2)}, u32[]{:S(2)}) collective-permute-start(bf16[256,2048]{1,0:T(8,128)(2,1)S(1)} %pad_maximum_fusion.1.first_ref), channel_id=1, source_target_pairs={{0,4},{1,9},{2,6},{3,11},{4,0},{5,13},{6,2},{7,15},{8,12},{9,1},{1... | collective-permute-start | bytes 3145736 | tf_op jit(solution)/shard_map/ppermute | solution.py:47
